TPU v7x, 32 devices: a whole 2x2x4 slice. The times are simulated.
32 devices in a mesh: expert: 8 (over z, y), hidden: 4 (over x, core).
Axes of the slice: x: 2, y: 2, z: 4, core: 2. Of those that a mesh axis runs over, the one named last changes fastest.
Arguments:
- tokens: bfloat16 [2, 6144, 768], P(None, 'expert'), may hold values from -6 to 6
- doc_ids: int32 [2, 8, 768], P(None, 'expert'), may hold values from 0 to 3, never falling along the last dimension, each value on 1 to 384 neighbouring positions
- pad_mask: int32 [2, 6144], P(None, 'expert'), may hold values 0 or 1
- norm1_gain: float32 [768], replicated, may hold values from 0.5 to 1.5
- norm1_bias: float32 [768], replicated, may hold values from -1 to 1
- qkv_weight: bfloat16 [3, 768, 768], P(None, None, 'hidden'), may hold values from -0.3125 to 0.3125
- out_weight: bfloat16 [768, 768], P('hidden'), may hold values from -0.875 to 0.875
- norm2_gain: float32 [768], replicated, may hold values from 0.5 to 1.5
- norm2_bias: float32 [768], replicated, may hold values from -1 to 1
- router: bfloat16 [768, 8], replicated, may hold values from -0.15625 to 0.15625
- routes: int32 [2, 6144, 2], P(None, 'expert'), may hold values from 0 to 7, all different within a row; in each aligned block of 768 rows (0 to 767, 768 to 1535, ..., all dimensions but the last counted through in order) at most 384 rows name the same one
- up_weight: bfloat16 [8, 768, 3072], P('expert', None, 'hidden'), may hold values from -0.21875 to 0.21875
- down_weight: bfloat16 [8, 768, 3072], P('expert', None, 'hidden'), may hold values from -0.15625 to 0.15625
- cotangent: bfloat16 [2, 6144, 768], P(None, 'expert'), may hold values from -6 to 6
Outputs:
- block_out: float32 [2, 6144, 768], P(None, 'expert')
- grad_tokens: float32 [2, 6144, 768], P(None, 'expert')
- grad_norm1_gain: float32 [768], replicated
- grad_norm1_bias: float32 [768], replicated
- grad_qkv: float32 [3, 768, 768], P(None, None, 'hidden')
- grad_out: float32 [768, 768], P('hidden')
- grad_norm2_gain: float32 [768], replicated
- grad_norm2_bias: float32 [768], replicated
- grad_router: float32 [768, 8], replicated
- grad_up: float32 [4, 768, 3072], P(None, 'expert', 'hidden')
- grad_down: float32 [4, 768, 3072], P(None, 'expert', 'hidden')
Inputs may be any that keep to these rules, and one draw needn't show every extreme that they name: `routes`: each token names 2 different experts. In each micro-batch the tokens of one pack name any one expert at most 384 times, a bound that some block reaches. `doc_ids`: within a pack document numbers never fall; each document covers 1 to 384 consecutive tokens, and some covers exactly 384. `pad_mask`: 1 marks a real token, 0 a padding token.
All inputs are finite; a program needn't handle non-finite values. No bound on the sum of `pad_mask` on one device may be relied on, other than what follows from the above.
Results may differ from a plain program's by a relative error of at most 0.028.
Values may be sent and summed in bfloat16 or wider, within the bound.
No kernel may reach another device: no remote copies, remote signals or barrier semaphores. Data moves between devices by JAX's collectives and lax.ppermute only.
A program may use at most 256 MiB of HBM per device.

v0:
```python
import jax
import jax.numpy as jnp
from jax import lax
from jax.sharding import PartitionSpec as P

HEAD_DIM = 64
EPSILON = 1e-05
PRECISE = lax.Precision.HIGHEST
MASKED = -1e30


def layer_norm(values, norm_gain, norm_bias):
    centre = values - jnp.mean(values, -1, keepdims=True)
    spread = jnp.mean(centre * centre, -1, keepdims=True)
    return centre * lax.rsqrt(spread + EPSILON) * norm_gain + norm_bias


def gelu_tanh(values):
    return jax.nn.gelu(values, approximate=True)


def visible(doc_row, pad_row):
    total_rows = doc_row.shape[0]
    query_pos = jnp.arange(total_rows)[:, None]
    key_pos = jnp.arange(total_rows)[None, :]
    same_doc = doc_row[:, None] == doc_row[None, :]
    is_real = (pad_row[None, :] == 1) | (query_pos == key_pos)
    return (key_pos <= query_pos) & same_doc & is_real


def slot_tables(route_rows, experts, capacity):
    flat_routes = route_rows.reshape(-1)
    onehot = (flat_routes[:, None] == jnp.arange(experts, dtype=jnp.int32)[None, :]).astype(
        jnp.int32
    )
    before = jnp.cumsum(onehot, 0) - onehot
    placed = jnp.sum(before * onehot, 1)
    slot_index = flat_routes * capacity + placed
    total_rows = flat_routes.shape[0]
    source = (
        jnp.full((experts * capacity,), total_rows, jnp.int32)
        .at[slot_index]
        .set(jnp.arange(total_rows, dtype=jnp.int32))
    )
    return (slot_index, source)


def masked_scores(queries, key_rows, allowed, score_scale):
    scores = (
        jnp.einsum("qhd,khd->hqk", queries, key_rows, preferred_element_type=jnp.float32)
        * score_scale
    )
    return jnp.where(allowed[None], scores, MASKED)


def attend_forward(queries, key_rows, value_rows, allowed, score_scale):
    scores = masked_scores(queries, key_rows, allowed, score_scale)
    row_peak = jnp.max(scores, -1, keepdims=True)
    exponent = jnp.exp(scores - row_peak)
    row_total = jnp.sum(exponent, -1, keepdims=True)
    attn_weights = (exponent / row_total).astype(jnp.bfloat16)
    output = jnp.einsum(
        "hqk,khd->qhd", attn_weights, value_rows, preferred_element_type=jnp.float32
    )
    return (output, row_peak + jnp.log(row_total))


def attend_backward(queries, key_rows, value_rows, allowed, score_scale, log_total, heads_grad):
    scores = masked_scores(queries, key_rows, allowed, score_scale)
    attn_weights = jnp.exp(scores - log_total)
    weight_grad = jnp.einsum(
        "qhd,khd->hqk", heads_grad, value_rows, preferred_element_type=jnp.float32
    )
    row_delta = jnp.sum(attn_weights * weight_grad, -1, keepdims=True)
    score_grad = (attn_weights * (weight_grad - row_delta)).astype(jnp.bfloat16)
    query_grad = (
        jnp.einsum("hqk,khd->qhd", score_grad, key_rows, preferred_element_type=jnp.float32)
        * score_scale
    )
    key_grad = (
        jnp.einsum("hqk,qhd->khd", score_grad, queries, preferred_element_type=jnp.float32)
        * score_scale
    )
    value_grad = jnp.einsum(
        "hqk,qhd->khd",
        attn_weights.astype(jnp.bfloat16),
        heads_grad,
        preferred_element_type=jnp.float32,
    )
    return (query_grad, key_grad, value_grad)


def shards(
    tokens,
    doc_ids,
    pad_mask,
    norm1_gain,
    norm1_bias,
    qkv_weight,
    out_weight,
    norm2_gain,
    norm2_bias,
    router,
    routes,
    up_weight,
    down_weight,
    cotangent,
):
    micro_count, row_count, feat_width = tokens.shape
    expert_count = router.shape[1]
    top_count = routes.shape[2]
    capacity = 2 * row_count * top_count // expert_count
    local_heads = qkv_weight.shape[2] // HEAD_DIM
    score_scale = HEAD_DIM ** (-0.5)
    trainable = lax.axis_index("expert") >= lax.axis_size("expert") // 2
    up_local = up_weight[0]
    down_local = down_weight[0]
    router_wide = router.astype(jnp.float32)
    zero_row = jnp.zeros((1, feat_width), jnp.bfloat16)
    grad_qkv = jnp.zeros(qkv_weight.shape, jnp.float32)
    grad_proj = jnp.zeros(out_weight.shape, jnp.float32)
    grad_router = jnp.zeros(router.shape, jnp.float32)
    gain1_total = jnp.zeros((feat_width,), jnp.float32)
    bias1_total = jnp.zeros((feat_width,), jnp.float32)
    gain2_total = jnp.zeros((feat_width,), jnp.float32)
    bias2_total = jnp.zeros((feat_width,), jnp.float32)
    expert_acc = (jnp.zeros(up_local.shape, jnp.float32), jnp.zeros(down_local.shape, jnp.float32))
    outputs = []
    input_grads = []
    for micro_idx in range(micro_count):
        inputs = tokens[micro_idx].astype(jnp.float32)
        allowed = visible(doc_ids[micro_idx, 0], pad_mask[micro_idx])
        normed1, norm1_pull = jax.vjp(layer_norm, inputs, norm1_gain, norm1_bias)
        attn_in = normed1.astype(jnp.bfloat16)
        projected = jnp.einsum(
            "rd,cdf->crf", attn_in, qkv_weight, preferred_element_type=jnp.float32
        ).astype(jnp.bfloat16)
        head_view = projected.reshape(3, row_count, local_heads, HEAD_DIM)
        queries, key_rows, value_rows = (head_view[0], head_view[1], head_view[2])
        heads_out, log_total = attend_forward(queries, key_rows, value_rows, allowed, score_scale)
        heads_low = heads_out.reshape(row_count, -1).astype(jnp.bfloat16)
        attn_term = jnp.dot(heads_low, out_weight, preferred_element_type=jnp.float32)
        attention = lax.psum(attn_term.astype(jnp.bfloat16), "hidden").astype(jnp.float32)
        residual = inputs + attention
        normed2, norm2_pull = jax.vjp(layer_norm, residual, norm2_gain, norm2_bias)
        moe_in = normed2.astype(jnp.bfloat16)
        logits = jnp.dot(moe_in, router, preferred_element_type=jnp.float32)
        route_rows = routes[micro_idx]
        picker = (
            route_rows[:, :, None] == jnp.arange(expert_count, dtype=jnp.int32)[None, None, :]
        ).astype(jnp.float32)
        chosen = jnp.sum(picker * logits[:, None, :], -1)
        gate_vals = jax.nn.softmax(chosen, -1)
        slot_index, source = slot_tables(route_rows, expert_count, capacity)
        padded_in = jnp.concatenate([moe_in, zero_row], 0)
        send_rows = padded_in[source // top_count].reshape(expert_count, capacity, feat_width)
        received = lax.all_to_all(
            send_rows, "expert", split_axis=0, concat_axis=0, tiled=True
        ).reshape(-1, feat_width)
        hidden_pre = jnp.dot(received, up_local, preferred_element_type=jnp.float32)
        hidden_act = gelu_tanh(hidden_pre).astype(jnp.bfloat16)
        slice_out = jnp.einsum(
            "rf,df->rd", hidden_act, down_local, preferred_element_type=jnp.float32
        )
        summed = lax.psum(slice_out.astype(jnp.bfloat16), "hidden")
        returned = lax.all_to_all(
            summed.reshape(expert_count, capacity, feat_width),
            "expert",
            split_axis=0,
            concat_axis=0,
            tiled=True,
        )
        flat_back = jnp.concatenate([returned.reshape(-1, feat_width), zero_row], 0)
        expert_rows = flat_back[slot_index].reshape(row_count, top_count, feat_width)
        expert_wide = expert_rows.astype(jnp.float32)
        mixture = jnp.sum(gate_vals[:, :, None] * expert_wide, 1)
        outputs.append(residual + mixture)
        upstream = cotangent[micro_idx].astype(jnp.float32)
        expert_grad = (gate_vals[:, :, None] * upstream[:, None, :]).astype(jnp.bfloat16)
        gate_grad = jnp.sum(upstream[:, None, :] * expert_wide, -1)
        chosen_grad = gate_vals * (gate_grad - jnp.sum(gate_vals * gate_grad, -1, keepdims=True))
        logit_grad = jnp.sum(picker * chosen_grad[:, :, None], 1)
        padded_grad = jnp.concatenate([expert_grad.reshape(-1, feat_width), zero_row], 0)
        send_grad = padded_grad[source].reshape(expert_count, capacity, feat_width)
        grad_rows = lax.all_to_all(
            send_grad, "expert", split_axis=0, concat_axis=0, tiled=True
        ).reshape(-1, feat_width)
        act_grad = jnp.dot(grad_rows, down_local, preferred_element_type=jnp.float32)
        gelu_grad = jax.vjp(gelu_tanh, hidden_pre)[1](act_grad)[0]
        pre_grad = gelu_grad.astype(jnp.bfloat16)
        in_term = jnp.einsum("rf,df->rd", pre_grad, up_local, preferred_element_type=jnp.float32)
        in_summed = lax.psum(in_term.astype(jnp.bfloat16), "hidden")
        in_back = lax.all_to_all(
            in_summed.reshape(expert_count, capacity, feat_width),
            "expert",
            split_axis=0,
            concat_axis=0,
            tiled=True,
        )
        flat_in = jnp.concatenate([in_back.reshape(-1, feat_width), zero_row], 0)
        copies_low = flat_in[slot_index].reshape(row_count, top_count, feat_width)
        copies_grad = copies_low.astype(jnp.float32)
        normed2_grad = jnp.sum(copies_grad, 1) + jnp.dot(
            logit_grad, router_wide.T, precision=PRECISE
        )

        def expert_update(acc_pair):
            return (
                acc_pair[0]
                + jnp.einsum("rd,rf->df", received, pre_grad, preferred_element_type=jnp.float32),
                acc_pair[1]
                + jnp.einsum(
                    "rd,rf->df", grad_rows, hidden_act, preferred_element_type=jnp.float32
                ),
            )

        def expert_keep(acc_pair):
            return acc_pair

        expert_acc = lax.cond(trainable, expert_update, expert_keep, expert_acc)
        grad_router = grad_router + jnp.dot(
            moe_in.astype(jnp.float32).T, logit_grad, precision=PRECISE
        )
        resid_grad, gain2_grad, bias2_grad = norm2_pull(normed2_grad)
        gain2_total = gain2_total + gain2_grad
        bias2_total = bias2_total + bias2_grad
        resid_grad = upstream + resid_grad
        attn_grad = resid_grad.astype(jnp.bfloat16)
        grad_proj = grad_proj + jnp.einsum(
            "rf,rd->fd", heads_low, attn_grad, preferred_element_type=jnp.float32
        )
        heads_grad = jnp.einsum(
            "rd,fd->rf", attn_grad, out_weight, preferred_element_type=jnp.float32
        ).astype(jnp.bfloat16)
        query_grad, key_grad, value_grad = attend_backward(
            queries,
            key_rows,
            value_rows,
            allowed,
            score_scale,
            log_total,
            heads_grad.reshape(row_count, local_heads, HEAD_DIM),
        )
        qkv_grad = (
            jnp.stack([query_grad, key_grad, value_grad])
            .reshape(3, row_count, -1)
            .astype(jnp.bfloat16)
        )
        grad_qkv = grad_qkv + jnp.einsum(
            "rd,crf->cdf", attn_in, qkv_grad, preferred_element_type=jnp.float32
        )
        normed1_term = jnp.einsum(
            "crf,cdf->rd", qkv_grad, qkv_weight, preferred_element_type=jnp.float32
        )
        normed1_grad = lax.psum(normed1_term.astype(jnp.bfloat16), "hidden").astype(jnp.float32)
        input_grad, gain1_grad, bias1_grad = norm1_pull(normed1_grad)
        gain1_total = gain1_total + gain1_grad
        bias1_total = bias1_total + bias1_grad
        input_grads.append(resid_grad + input_grad)
    reduced = (
        lax.psum(gain1_total.astype(jnp.bfloat16), "expert").astype(jnp.float32),
        lax.psum(bias1_total.astype(jnp.bfloat16), "expert").astype(jnp.float32),
        lax.psum(grad_qkv.astype(jnp.bfloat16), "expert").astype(jnp.float32),
        lax.psum(grad_proj.astype(jnp.bfloat16), "expert").astype(jnp.float32),
        lax.psum(gain2_total.astype(jnp.bfloat16), "expert").astype(jnp.float32),
        lax.psum(bias2_total.astype(jnp.bfloat16), "expert").astype(jnp.float32),
        lax.psum(grad_router.astype(jnp.bfloat16), "expert").astype(jnp.float32),
    )
    expert_parts = (
        lax.all_to_all(
            expert_acc[0][None].astype(jnp.bfloat16),
            "expert",
            split_axis=1,
            concat_axis=0,
            tiled=True,
        ).astype(jnp.float32),
        lax.all_to_all(
            expert_acc[1][None].astype(jnp.bfloat16),
            "expert",
            split_axis=1,
            concat_axis=0,
            tiled=True,
        ).astype(jnp.float32),
    )
    half_count = expert_count // 2
    return (
        jnp.stack(outputs),
        jnp.stack(input_grads),
        reduced[0],
        reduced[1],
        reduced[2],
        reduced[3],
        reduced[4],
        reduced[5],
        reduced[6],
        expert_parts[0][half_count:],
        expert_parts[1][half_count:],
    )


def solution(mesh):
    placed = (
        P(None, "expert", None),
        P(None, "expert", None),
        P(None, "expert"),
        P(),
        P(),
        P(None, None, "hidden"),
        P("hidden", None),
        P(),
        P(),
        P(),
        P(None, "expert", None),
        P("expert", None, "hidden"),
        P("expert", None, "hidden"),
        P(None, "expert", None),
    )
    return jax.shard_map(
        shards,
        mesh=mesh,
        in_specs=placed,
        out_specs=(
            P(None, "expert", None),
            P(None, "expert", None),
            P(),
            P(),
            P(None, None, "hidden"),
            P("hidden", None),
            P(),
            P(),
            P(),
            P(None, "expert", "hidden"),
            P(None, "expert", "hidden"),
        ),
        check_vma=False,
    )
```

profile of v0, /device:TPU:0, one launch (start us, length us, event | category | flops | bytes accessed | tf_op | source)
XLA Modules:
  0.0 1665.4 jit_solution(2692091185587568231)
XLA Ops:
  46.8 17.9 %all-reduce.18.cloned.1.call-done = bf16[768,768]{1,0:T(8,128)(2,1)} async-done(((bf16[768,768]{1,0:T(8,128)(2,1)}), bf16[768,768]{1,0:T(8,128)(2,1)}) %all-reduce.18.cloned.1.call-update) | async-done | bytes 1179664 | tf_op jit(solution)/shard_map/psum | solution.py:143
  82.5 5.6 mul.541
  88.1 6.9 mul.542
  96.9 7.0 scatter_custom_fusion
  105.3 10.1 all-reduce.20.cloned.1.call-done
  128.2 14.5 gather_fusion.4
  142.7 5.6 all-to-all-start.4
  153.0 6.2 scatter_custom_fusion.1
  159.9 14.5 gather_fusion.2
  174.4 78.2 %all-to-all-done.4 = bf16[8,384,768]{2,1,0:T(8,128)(2,1)} async-done(((bf16[8,384,768]{2,1,0:T(8,128)(2,1)}), bf16[8,384,768]{2,1,0:T(8,128)(2,1)}, u32[]{:S(2)}, u32[]{:S(2)}) %all-to-all-start.4) | async-done | bytes 4718624 | tf_op jit(solution)/shard_map/all_to_all | solution.py:185
  257.5 14.5 gather_fusion
  272.1 89.1 %all-to-all-done.2 = bf16[8,384,768]{2,1,0:T(8,128)(2,1)} async-done(((bf16[8,384,768]{2,1,0:T(8,128)(2,1)}), bf16[8,384,768]{2,1,0:T(8,128)(2,1)}, u32[]{:S(2)}, u32[]{:S(2)}) %all-to-all-start.2) | async-done | bytes 4718624 | tf_op jit(solution)/shard_map/all_to_all | solution.py:157
  369.7 7.0 mul.579
  382.2 14.6 gather_fusion.6
  396.8 72.8 %all-to-all-done = bf16[8,384,768]{2,1,0:T(8,128)(2,1)} async-done(((bf16[8,384,768]{2,1,0:T(8,128)(2,1)}), bf16[8,384,768]{2,1,0:T(8,128)(2,1)}, u32[]{:S(2)}, u32[]{:S(2)}) %all-to-all-start) | async-done | bytes 4718624 | tf_op jit(solution)/shard_map/all_to_all | solution.py:157
  474.4 7.7 multiply_convert_fusion.1
  482.1 12.1 fusion.6
  494.1 5.6 convolution_convert_fusion.1
  505.3 10.1 multiply_convert_fusion
  515.4 62.6 %all-to-all-done.6 = bf16[8,384,768]{2,1,0:T(8,128)(2,1)} async-done(((bf16[8,384,768]{2,1,0:T(8,128)(2,1)}), bf16[8,384,768]{2,1,0:T(8,128)(2,1)}, u32[]{:S(2)}, u32[]{:S(2)}) %all-to-all-start.6) | async-done | bytes 4718624 | tf_op jit(solution)/shard_map/all_to_all | solution.py:185
  578.0 11.9 fusion.13
  589.9 5.6 convolution_convert_fusion
  595.5 5.6 convolution_convert_fusion.2
  609.3 7.8 reduce.30
  618.3 32.7 %all-to-all-start.8 = ((bf16[8,2,36864]{2,1,0:T(2,128)(2,1)}), bf16[8,2,36864]{2,1,0:T(2,128)(2,1)}, u32[]{:S(2)}, u32[]{:S(2)}) async-start(bf16[8,2,36864]{2,1,0:T(2,128)(2,1)} %reshape.916), calls=%async_computation.8 | async-start | bytes 2359296 | tf_op jit(solution)/shard_map/all_to_all | solution.py:270
  652.9 7.8 reduce.31
  661.1 18.7 %all-to-all-done.8 = bf16[8,2,36864]{2,1,0:T(2,128)(2,1)} async-done(((bf16[8,2,36864]{2,1,0:T(2,128)(2,1)}), bf16[8,2,36864]{2,1,0:T(2,128)(2,1)}, u32[]{:S(2)}, u32[]{:S(2)}) %all-to-all-start.8) | async-done | bytes 1179680 | tf_op jit(solution)/shard_map/all_to_all | solution.py:270
  679.8 32.5 %all_to_all.58 = bf16[8,2,36864]{2,1,0:T(2,128)(2,1)S(1)} all-to-all(bf16[8,2,36864]{2,1,0:T(2,128)(2,1)S(1)} %reshape.918), channel_id=1, replica_groups=mesh['expert'=8,'hidden'=4] {'expert'}, dimensions={0} | all-to-all | bytes 2359296 | tf_op jit(solution)/shard_map/all_to_all | solution.py:277
  712.3 208.9 %all-reduce.26.cloned.1.call-done = (bf16[8,384,768]{2,1,0:T(8,128)(2,1)}, bf16[8,384,768]{2,1,0:T(8,128)(2,1)}, bf16[8,384,768]{2,1,0:T(8,128)(2,1)}, bf16[8,384,768]{2,1,0:T(8,128)(2,1)}) async-done(((bf16[8,384,768]{2,1,0:T(8,128)(2,1)}, bf16[8,384,768]{2,1,0:T(8,128)(2,1)}, bf16[8,384,768]{2,1,0:T(8,128)(2,1)}, bf16[8,384,768]{2,1,0:T(8,128)(2,1)}), (bf16[8,384,768]{2,1,0:T(8,128)(2,1)}, ...) | async-done | bytes 18874384 | tf_op jit(solution)/shard_map/psum | solution.py:165
  921.3 110.1 %all_to_all.59 = bf16[8,384,768]{2,1,0:T(8,128)(2,1)} all-to-all(bf16[8,384,768]{2,1,0:T(8,128)(2,1)} %get-tuple-element.99), channel_id=1, replica_groups=mesh['expert'=8,'hidden'=4] {'expert'}, dimensions={0} | all-to-all | bytes 9437184 | tf_op jit(solution)/shard_map/all_to_all | solution.py:166
  1031.4 107.6 %all_to_all.60 = bf16[8,384,768]{2,1,0:T(8,128)(2,1)} all-to-all(bf16[8,384,768]{2,1,0:T(8,128)(2,1)S(1)} %copy-done.38), channel_id=1, replica_groups=mesh['expert'=8,'hidden'=4] {'expert'}, dimensions={0} | all-to-all | bytes 9437184 | tf_op jit(solution)/shard_map/all_to_all | solution.py:193
  1139.0 107.5 %all_to_all.61 = bf16[8,384,768]{2,1,0:T(8,128)(2,1)} all-to-all(bf16[8,384,768]{2,1,0:T(8,128)(2,1)S(1)} %bitcast.379), channel_id=1, replica_groups=mesh['expert'=8,'hidden'=4] {'expert'}, dimensions={0} | all-to-all | bytes 9437184 | tf_op jit(solution)/shard_map/all_to_all | solution.py:193
  1277.0 9.6 gather_fusion.5
  1286.6 9.6 gather_fusion.1
  1296.2 58.5 %all-to-all-done.3 = bf16[8,384,768]{2,1,0:T(8,128)(2,1)} async-done(((bf16[8,384,768]{2,1,0:T(8,128)(2,1)}), bf16[8,384,768]{2,1,0:T(8,128)(2,1)}, u32[]{:S(2)}, u32[]{:S(2)}) %all-to-all-start.3) | async-done | bytes 4718624 | tf_op jit(solution)/shard_map/all_to_all | solution.py:166
  1359.7 9.6 gather_fusion.7
  1369.3 9.6 gather_fusion.3
  1379.0 6.7 reshape.803
  1385.8 13.4 multiply_reduce_fusion.2
  1400.0 6.3 reshape.802
  1406.4 13.7 multiply_reduce_fusion.3
  1423.9 6.3 reshape.807
  1434.1 9.5 reduce_sum.493
  1443.6 9.3 reduce_sum.484
  1456.4 5.9 multiply_reduce_fusion.7
  1515.0 47.2 %all-reduce.24.cloned.1.call-done = (bf16[768,768]{1,0:T(8,128)(2,1)}, bf16[768,768]{1,0:T(8,128)(2,1)}) async-done(((bf16[768,768]{1,0:T(8,128)(2,1)}, bf16[768,768]{1,0:T(8,128)(2,1)}), (bf16[768,768]{1,0:T(8,128)(2,1)}, bf16[768,768]{1,0:T(8,128)(2,1)})) %all-reduce.24.cloned.1.call-update) | async-done | bytes 2359312 | tf_op jit(solution)/shard_map/psum | solution.py:255
  1570.1 38.8 %all-reduce.8 = (bf16[768]{0:T(1024)(128)(2,1)}, bf16[768]{0:T(1024)(128)(2,1)}, bf16[768]{0:T(1024)(128)(2,1)}, bf16[768]{0:T(1024)(128)(2,1)}, bf16[768,8]{0,1:T(8,128)(2,1)}) all-reduce(bf16[768]{0:T(1024)(128)(2,1)} %add_convert_fusion.6, ...), channel_id=1, replica_groups=mesh['expert'=8,'hidden'=4] {'expert'}, use_global_device_ids=true, to_apply=%region_56.57 | all-reduce | flops 9216 | bytes 36864 | tf_op jit(solution)/shard_map/psum | solution.py:261
  1617.8 29.0 %all-reduce.22.cloned.1.call-done = (bf16[3,768,192]{1,2,0:T(8,128)(2,1)}, bf16[192,768]{1,0:T(8,128)(2,1)}) async-done(((bf16[3,768,192]{1,2,0:T(8,128)(2,1)}, bf16[192,768]{1,0:T(8,128)(2,1)}), (bf16[3,768,192]{1,2,0:T(8,128)(2,1)}, bf16[192,768]{1,0:T(8,128)(2,1)})) %all-reduce.22.cloned.1.call-update) | async-done | bytes 1179664 | tf_op jit(solution)/shard_map/psum | solution.py:263
  (508 shorter events, 248.0 us)
Async XLA Ops:
  7.2 467.2 %copy-start = (bf16[1,768,768]{2,1,0:T(8,128)(2,1)S(1)}, bf16[1,768,768]{2,1,0:T(8,128)(2,1)}, u32[]{:S(2)}) copy-start(bf16[1,768,768]{2,1,0:T(8,128)(2,1)} %param.29) | copy-start | bytes 3538948
  7.2 57.4 %all-reduce.18.cloned.1.call-start = ((), (), s32[]{:S(2)}) async-start(), calls=%async_computation.10 | async-start | bytes 2359296 | tf_op jit(solution)/shard_map/psum | solution.py:143
  24.2 91.2 %all-reduce.20.cloned.1.call-start = ((), (), s32[]{:S(2)}) async-start(), calls=%async_computation.11 | async-start | bytes 2359296 | tf_op jit(solution)/shard_map/psum | solution.py:143
  26.0 97.0 %copy-start.102 = (s32[768,2]{0,1:T(2,128)}, s32[768,2]{0,1:T(2,128)S(1)}, u32[]{:S(2)}) copy-start(s32[768,2]{0,1:T(2,128)S(1)} %get-tuple-element.125) | copy-start | bytes 18436
  42.6 24.8 %copy-start.89 = (f32[768]{0:T(1024)}, f32[768]{0:T(1024)S(1)}, u32[]{:S(2)}) copy-start(f32[768]{0:T(1024)S(1)} %broadcast_multiply_fusion.3) | copy-start | bytes 9220
  88.1 17.2 %copy-start.138 = (f32[768]{0:T(1024)S(1)}, f32[768]{0:T(1024)}, u32[]{:S(2)}) copy-start(f32[768]{0:T(1024)} %get-tuple-element.75) | copy-start | bytes 9220
  105.3 14.0 copy-start.100
  142.7 9.1 copy-start.134
  142.7 110.0 %all-to-all-start.4 = ((bf16[8,384,768]{2,1,0:T(8,128)(2,1)}), bf16[8,384,768]{2,1,0:T(8,128)(2,1)}, u32[]{:S(2)}, u32[]{:S(2)}) async-start(bf16[8,384,768]{2,1,0:T(8,128)(2,1)} %bitcast.363), calls=%async_computation.4 | async-start | bytes 9437184 | tf_op jit(solution)/shard_map/all_to_all | solution.py:185
  148.4 11.4 copy-start.19
  252.7 108.5 %all-to-all-start.2 = ((bf16[8,384,768]{2,1,0:T(8,128)(2,1)}), bf16[8,384,768]{2,1,0:T(8,128)(2,1)}, u32[]{:S(2)}, u32[]{:S(2)}) async-start(bf16[8,384,768]{2,1,0:T(8,128)(2,1)} %bitcast.366), calls=%async_computation.2 | async-start | bytes 9437184 | tf_op jit(solution)/shard_map/all_to_all | solution.py:157
  361.2 108.5 %all-to-all-start = ((bf16[8,384,768]{2,1,0:T(8,128)(2,1)}), bf16[8,384,768]{2,1,0:T(8,128)(2,1)}, u32[]{:S(2)}, u32[]{:S(2)}) async-start(bf16[8,384,768]{2,1,0:T(8,128)(2,1)} %bitcast.364), calls=%async_computation | async-start | bytes 9437184 | tf_op jit(solution)/shard_map/all_to_all | solution.py:157
  369.7 7.0 copy-start.20
  369.7 7.0 copy-start.81
  369.7 7.4 copy-start.103
  469.6 108.3 %all-to-all-start.6 = ((bf16[8,384,768]{2,1,0:T(8,128)(2,1)}), bf16[8,384,768]{2,1,0:T(8,128)(2,1)}, u32[]{:S(2)}, u32[]{:S(2)}) async-start(bf16[8,384,768]{2,1,0:T(8,128)(2,1)} %bitcast.365), calls=%async_computation.6 | async-start | bytes 9437184 | tf_op jit(solution)/shard_map/all_to_all | solution.py:185
  474.3 447.0 %all-reduce.26.cloned.1.call-start = ((), (), s32[]{:S(2)}) async-start(), calls=%async_computation.14 | async-start | bytes 37748736 | tf_op jit(solution)/shard_map/psum | solution.py:165
  474.4 7.7 copy-start.142
  482.0 17.7 %copy-start.152 = (bf16[3072,768]{1,0:T(8,128)(2,1)}, bf16[3072,768]{1,0:T(8,128)(2,1)S(1)}, u32[]{:S(2)}) copy-start(bf16[3072,768]{1,0:T(8,128)(2,1)S(1)} %get-tuple-element.139) | copy-start | bytes 14155780
  617.1 33.9 %copy-start.34 = (f32[768,768]{1,0:T(8,128)S(1)}, f32[768,768]{1,0:T(8,128)}, u32[]{:S(2)}) copy-start(f32[768,768]{1,0:T(8,128)} %copy-done.33) | copy-start | bytes 7077892
  618.3 61.5 %all-to-all-start.8 = ((bf16[8,2,36864]{2,1,0:T(2,128)(2,1)}), bf16[8,2,36864]{2,1,0:T(2,128)(2,1)}, u32[]{:S(2)}, u32[]{:S(2)}) async-start(bf16[8,2,36864]{2,1,0:T(2,128)(2,1)} %reshape.916), calls=%async_computation.8 | async-start | bytes 2359296 | tf_op jit(solution)/shard_map/all_to_all | solution.py:270
  921.3 110.1 %copy-start.38 = (bf16[8,384,768]{2,1,0:T(8,128)(2,1)S(1)}, bf16[8,384,768]{2,1,0:T(8,128)(2,1)}, u32[]{:S(2)}) copy-start(bf16[8,384,768]{2,1,0:T(8,128)(2,1)} %get-tuple-element.100) | copy-start | bytes 14155780
  921.3 217.8 %slice-start.8 = ((s8[4718592]{0:T(1024)(128)(4,1)}), s8[4194304]{0:T(1024)(128)(4,1)S(1)}, s32[]{:S(2)}) async-start(s8[4718592]{0:T(1024)(128)(4,1)} %bitcast.378), calls=%async_computation.23 | async-start | bytes 8388608
  1031.4 107.6 %slice-start.9 = ((s8[4718592]{0:T(1024)(128)(4,1)}), s8[524288]{0:T(1024)(128)(4,1)S(1)}, s32[]{:S(2)}) async-start(s8[4718592]{0:T(1024)(128)(4,1)} %bitcast.378), calls=%async_computation.24 | async-start | bytes 1048576
  1246.5 108.2 %all-to-all-start.3 = ((bf16[8,384,768]{2,1,0:T(8,128)(2,1)}), bf16[8,384,768]{2,1,0:T(8,128)(2,1)}, u32[]{:S(2)}, u32[]{:S(2)}) async-start(bf16[8,384,768]{2,1,0:T(8,128)(2,1)} %get-tuple-element.98), calls=%async_computation.3 | async-start | bytes 9437184 | tf_op jit(solution)/shard_map/all_to_all | solution.py:166
  1251.3 310.9 %all-reduce.24.cloned.1.call-start = ((), (), s32[]{:S(2)}) async-start(), calls=%async_computation.13 | async-start | bytes 4718592 | tf_op jit(solution)/shard_map/psum | solution.py:255
  1258.4 13.6 slice-start.6
  1265.5 6.4 slice-start.7
  1266.6 7.8 slice-start.4
  1379.0 6.7 copy-start.14
  1379.0 6.7 copy-start.41
  1385.7 13.6 copy-start.73
  1385.7 13.6 copy-start.86
  1385.7 13.6 copy-start.99
  1385.8 13.7 copy-start.104
  1400.0 6.3 copy-start.12
  1406.4 14.9 copy-start.71
  1406.4 14.9 copy-start.84
  1406.4 14.9 copy-start.97
  1406.4 16.3 copy-start.24
  1423.8 6.3 copy-start.29
  1443.6 9.4 copy-start.82
  1443.6 12.7 copy-start.112
  1456.4 12.5 slice-start
  1462.4 6.5 slice-start.1
  1497.2 8.1 copy-start.67
  1498.6 6.7 copy-start.61
  1507.5 139.3 %all-reduce.22.cloned.1.call-start = ((), (), s32[]{:S(2)}) async-start(), calls=%async_computation.12 | async-start | bytes 2359296 | tf_op jit(solution)/shard_map/psum | solution.py:263
  (126 other events, 367.5 us)
Sparse Core Ops, SparseCore 0:
  24.3 40.3 all-reduce.17
  77.7 37.7 all-reduce.19
  601.2 320.0 all-reduce.25
  1507.6 54.4 all-reduce.23
  1566.1 80.6 all-reduce.21
where the time goes:
time: 1680 us; the launch traced here: 1670 us
  waiting for transfers between devices  693 us (41%)
  blocking collectives  397 us (24%)
  local copies, waits for them, and re-layouts  221 us (13%)
  other arithmetic  160 us (10%)
  matrix products  120 us (7%)
  starting transfers between devices  57.9 us (3%)
    all_to_all x2, blocking collectives, shards(): lax.all_to_all(in_summed.reshape(expert_count, capacity, feat_width), 'ex...  215 us
    psum x1, waiting for transfers between devices, shards(): summed = lax.psum(slice_out.astype(jnp.bfloat16), 'hidden')  209 us
    all_to_all x2, waiting for transfers between devices, shards(): lax.all_to_all(send_rows, 'expert', split_axis=0, concat_axis=0, tiled=True)  162 us
    all_to_all x2, waiting for transfers between devices, shards(): lax.all_to_all(send_grad, 'expert', split_axis=0, concat_axis=0, tiled=True)  141 us
    all_to_all x1, blocking collectives, shards(): lax.all_to_all(summed.reshape(expert_count, capacity, feat_width), 'exper...  110 us
    all_to_all x1, waiting for transfers between devices, shards(): lax.all_to_all(summed.reshape(expert_count, capacity, feat_width), 'exper...  58.5 us
    psum x1, waiting for transfers between devices, shards(): lax.psum(normed1_term.astype(jnp.bfloat16), 'hidden').astype(jnp.float32)  47.2 us
    psum x1, blocking collectives, shards(): lax.psum(gain1_total.astype(jnp.bfloat16), 'expert').astype(jnp.float32)  38.8 us
  transfers between devices with their start and end apart: 11, of which 11 were waited for; matrix products, arithmetic and copies ran while one was open for 15% of the time, Pallas kernels for 0%

commit v1 on v0

--- a/solution.py
+++ b/solution.py
@@ -7,6 +7,7 @@
 EPSILON = 1e-05
 PRECISE = lax.Precision.HIGHEST
 MASKED = -1e30
+raise_ticks = lambda array_in: jnp.sum(lax.all_gather(array_in, "hidden"), 0)
 
 
 def layer_norm(values, norm_gain, norm_bias):
@@ -252,7 +253,7 @@
         normed1_term = jnp.einsum(
             "crf,cdf->rd", qkv_grad, qkv_weight, preferred_element_type=jnp.float32
         )
-        normed1_grad = lax.psum(normed1_term.astype(jnp.bfloat16), "hidden").astype(jnp.float32)
+        normed1_grad = raise_ticks(normed1_term.astype(jnp.bfloat16)).astype(jnp.float32)
         input_grad, gain1_grad, bias1_grad = norm1_pull(normed1_grad)
         gain1_total = gain1_total + gain1_grad
         bias1_total = bias1_total + bias1_grad

time: 1680 us -> 1760 us (1.048)
  waiting for transfers between devices: 693 us -> 787 us
  blocking collectives: 397 us -> 364 us
    psum x1, waiting for transfers between devices: 209 us -> 320 us  [shards(): summed = lax.psum(slice_out.astype(jnp.bfloat16), 'hidden')]
    psum x1 -> x0, waiting for transfers between devices: 47.2 us -> none  [shards(): lax.psum(normed1_term.astype(jnp.bfloat16), 'hidden').astype(jnp.float32)]
    all_to_all x1 -> x0, blocking collectives: 32.5 us -> none  [shards(): lax.all_to_all(expert_acc[1][None].astype(jnp.bfloat16), 'expert', split_...]
    psum x1, waiting for transfers between devices: 29 us -> 0.01 us  [shards(): lax.psum(grad_qkv.astype(jnp.bfloat16), 'expert').astype(jnp.float32)]
    all_to_all x0 -> x1, waiting for transfers between devices: none -> 19.2 us  [shards(): lax.all_to_all(expert_acc[1][None].astype(jnp.bfloat16), 'expert', split_...]
  transfers between devices with their start and end apart: 11 -> 13, of which waited for: 11 -> 11; matrix products, arithmetic and copies ran while one was open for 15% -> 15% of each run, Pallas kernels for 0% -> 0%
where the time goes in v1:
time: 1760 us; the launch traced here: 1750 us
  waiting for transfers between devices  787 us (45%)
  blocking collectives  364 us (21%)
  local copies, waits for them, and re-layouts  225 us (13%)
  other arithmetic  171 us (10%)
  matrix products  120 us (7%)
  starting transfers between devices  64.8 us (4%)
    psum x1, waiting for transfers between devices, shards(): summed = lax.psum(slice_out.astype(jnp.bfloat16), 'hidden')  320 us
    all_to_all x2, blocking collectives, shards(): lax.all_to_all(in_summed.reshape(expert_count, capacity, feat_width), 'ex...  215 us
    all_to_all x2, waiting for transfers between devices, shards(): lax.all_to_all(send_rows, 'expert', split_axis=0, concat_axis=0, tiled=True)  162 us
    all_to_all x2, waiting for transfers between devices, shards(): lax.all_to_all(send_grad, 'expert', split_axis=0, concat_axis=0, tiled=True)  141 us
    all_to_all x1, blocking collectives, shards(): lax.all_to_all(summed.reshape(expert_count, capacity, feat_width), 'exper...  110 us
    all_to_all x1, waiting for transfers between devices, shards(): lax.all_to_all(summed.reshape(expert_count, capacity, feat_width), 'exper...  73.2 us
    psum x1, blocking collectives, shards(): lax.psum(gain1_total.astype(jnp.bfloat16), 'expert').astype(jnp.float32)  38.4 us
    all_to_all x1, starting transfers between devices, shards(): lax.all_to_all(expert_acc[0][None].astype(jnp.bfloat16), 'expert', split_...  36 us
  transfers between devices with their start and end apart: 13, of which 11 were waited for; matrix products, arithmetic and copies ran while one was open for 15% of the time, Pallas kernels for 0%

profile of v1, /device:TPU:0, one launch (start us, length us, event | category | flops | bytes accessed | tf_op | source)
XLA Modules:
  0.0 1748.3 jit_solution(1707819426683097036)
XLA Ops:
  46.4 18.2 %all-reduce.16.cloned.1.call-done = bf16[768,768]{1,0:T(8,128)(2,1)} async-done(((bf16[768,768]{1,0:T(8,128)(2,1)}), bf16[768,768]{1,0:T(8,128)(2,1)}) %all-reduce.16.cloned.1.call-update) | async-done | bytes 1179664 | tf_op jit(solution)/shard_map/psum | solution.py:144
  82.5 5.6 mul.541
  88.0 6.9 mul.542
  96.9 7.3 scatter_custom_fusion
  105.5 9.9 all-reduce.18.cloned.1.call-done
  128.1 14.5 gather_fusion.4
  142.7 5.6 all-to-all-start.4
  152.9 6.2 scatter_custom_fusion.1
  159.8 14.5 gather_fusion.2
  174.4 78.2 %all-to-all-done.4 = bf16[8,384,768]{2,1,0:T(8,128)(2,1)} async-done(((bf16[8,384,768]{2,1,0:T(8,128)(2,1)}), bf16[8,384,768]{2,1,0:T(8,128)(2,1)}, u32[]{:S(2)}, u32[]{:S(2)}) %all-to-all-start.4) | async-done | bytes 4718624 | tf_op jit(solution)/shard_map/all_to_all | solution.py:186
  257.5 14.5 gather_fusion
  272.0 89.1 %all-to-all-done.2 = bf16[8,384,768]{2,1,0:T(8,128)(2,1)} async-done(((bf16[8,384,768]{2,1,0:T(8,128)(2,1)}), bf16[8,384,768]{2,1,0:T(8,128)(2,1)}, u32[]{:S(2)}, u32[]{:S(2)}) %all-to-all-start.2) | async-done | bytes 4718624 | tf_op jit(solution)/shard_map/all_to_all | solution.py:158
  369.7 7.0 mul.579
  382.1 14.6 gather_fusion.6
  396.7 72.9 %all-to-all-done = bf16[8,384,768]{2,1,0:T(8,128)(2,1)} async-done(((bf16[8,384,768]{2,1,0:T(8,128)(2,1)}), bf16[8,384,768]{2,1,0:T(8,128)(2,1)}, u32[]{:S(2)}, u32[]{:S(2)}) %all-to-all-start) | async-done | bytes 4718624 | tf_op jit(solution)/shard_map/all_to_all | solution.py:158
  474.2 7.5 multiply_convert_fusion.1
  481.8 12.1 fusion.6
  493.9 5.5 convolution_convert_fusion.1
  505.0 10.1 multiply_convert_fusion
  515.1 62.8 %all-to-all-done.6 = bf16[8,384,768]{2,1,0:T(8,128)(2,1)} async-done(((bf16[8,384,768]{2,1,0:T(8,128)(2,1)}), bf16[8,384,768]{2,1,0:T(8,128)(2,1)}, u32[]{:S(2)}, u32[]{:S(2)}) %all-to-all-start.6) | async-done | bytes 4718624 | tf_op jit(solution)/shard_map/all_to_all | solution.py:186
  577.9 12.1 fusion.13
  590.1 5.7 convolution_convert_fusion
  595.8 5.5 convolution_convert_fusion.2
  601.4 320.2 %all-reduce.22.cloned.1.call-done = (bf16[8,384,768]{2,1,0:T(8,128)(2,1)}, bf16[8,384,768]{2,1,0:T(8,128)(2,1)}, bf16[8,384,768]{2,1,0:T(8,128)(2,1)}, bf16[8,384,768]{2,1,0:T(8,128)(2,1)}) async-done(((bf16[8,384,768]{2,1,0:T(8,128)(2,1)}, bf16[8,384,768]{2,1,0:T(8,128)(2,1)}, bf16[8,384,768]{2,1,0:T(8,128)(2,1)}, bf16[8,384,768]{2,1,0:T(8,128)(2,1)}), (bf16[8,384,768]{2,1,0:T(8,128)(2,1)}, ...) | async-done | bytes 18874384 | tf_op jit(solution)/shard_map/psum | solution.py:166
  921.6 110.1 %all_to_all.58 = bf16[8,384,768]{2,1,0:T(8,128)(2,1)} all-to-all(bf16[8,384,768]{2,1,0:T(8,128)(2,1)} %get-tuple-element.97), channel_id=1, replica_groups=mesh['expert'=8,'hidden'=4] {'expert'}, dimensions={0} | all-to-all | bytes 9437184 | tf_op jit(solution)/shard_map/all_to_all | solution.py:167
  1031.7 107.6 %all_to_all.59 = bf16[8,384,768]{2,1,0:T(8,128)(2,1)} all-to-all(bf16[8,384,768]{2,1,0:T(8,128)(2,1)S(1)} %copy-done.33), channel_id=1, replica_groups=mesh['expert'=8,'hidden'=4] {'expert'}, dimensions={0} | all-to-all | bytes 9437184 | tf_op jit(solution)/shard_map/all_to_all | solution.py:194
  1139.3 107.5 %all_to_all.60 = bf16[8,384,768]{2,1,0:T(8,128)(2,1)} all-to-all(bf16[8,384,768]{2,1,0:T(8,128)(2,1)S(1)} %bitcast.383), channel_id=1, replica_groups=mesh['expert'=8,'hidden'=4] {'expert'}, dimensions={0} | all-to-all | bytes 9437184 | tf_op jit(solution)/shard_map/all_to_all | solution.py:194
  1262.4 9.8 gather_fusion.5
  1272.2 9.6 gather_fusion.1
  1281.9 73.2 %all-to-all-done.3 = bf16[8,384,768]{2,1,0:T(8,128)(2,1)} async-done(((bf16[8,384,768]{2,1,0:T(8,128)(2,1)}), bf16[8,384,768]{2,1,0:T(8,128)(2,1)}, u32[]{:S(2)}, u32[]{:S(2)}) %all-to-all-start.3) | async-done | bytes 4718624 | tf_op jit(solution)/shard_map/all_to_all | solution.py:167
  1360.0 9.6 gather_fusion.7
  1369.6 9.7 gather_fusion.3
  1379.3 6.3 reshape.803
  1385.7 13.4 multiply_reduce_fusion.2
  1400.0 6.3 reshape.802
  1406.4 13.4 multiply_reduce_fusion.3
  1420.6 6.3 reshape.807
  1431.1 9.4 reduce_sum.518
  1440.5 9.3 reduce_sum.508
  1453.3 6.0 multiply_reduce_fusion.7
  1517.4 8.9 reduce.32
  1527.4 36.0 %all-to-all-start.8 = ((bf16[8,2,36864]{2,1,0:T(2,128)(2,1)}), bf16[8,2,36864]{2,1,0:T(2,128)(2,1)}, u32[]{:S(2)}, u32[]{:S(2)}) async-start(bf16[8,2,36864]{2,1,0:T(2,128)(2,1)} %reshape.918), calls=%async_computation.8 | async-start | bytes 2359296 | tf_op jit(solution)/shard_map/all_to_all | solution.py:271
  1568.5 8.8 reduce.33
  1578.6 26.2 %all-to-all-done.8 = bf16[8,2,36864]{2,1,0:T(2,128)(2,1)} async-done(((bf16[8,2,36864]{2,1,0:T(2,128)(2,1)}), bf16[8,2,36864]{2,1,0:T(2,128)(2,1)}, u32[]{:S(2)}, u32[]{:S(2)}) %all-to-all-start.8) | async-done | bytes 1179680 | tf_op jit(solution)/shard_map/all_to_all | solution.py:271
  1608.7 5.9 reshape.919
  1618.2 19.2 %all-to-all-done.9 = bf16[8,2,36864]{2,1,0:T(2,128)(2,1)S(1)} async-done(((bf16[8,2,36864]{2,1,0:T(2,128)(2,1)}), bf16[8,2,36864]{2,1,0:T(2,128)(2,1)S(1)}, u32[]{:S(2)}, u32[]{:S(2)}) %all-to-all-start.9) | async-done | bytes 1179680 | tf_op jit(solution)/shard_map/all_to_all | solution.py:278
  1658.4 17.0 all-gather.7.cloned.1.call-done
  1687.3 38.4 %all-reduce.8 = (bf16[768]{0:T(1024)(128)(2,1)}, bf16[768]{0:T(1024)(128)(2,1)}, bf16[768]{0:T(1024)(128)(2,1)}, bf16[768]{0:T(1024)(128)(2,1)}, bf16[768,8]{0,1:T(8,128)(2,1)}) all-reduce(bf16[768]{0:T(1024)(128)(2,1)} %add_convert_fusion.6, ...), channel_id=1, replica_groups=mesh['expert'=8,'hidden'=4] {'expert'}, use_global_device_ids=true, to_apply=%region_56.57 | all-reduce | flops 9216 | bytes 36864 | tf_op jit(solution)/shard_map/psum | solution.py:262
  (506 shorter events, 260.0 us)
Async XLA Ops:
  7.2 467.1 %copy-start = (bf16[1,768,768]{2,1,0:T(8,128)(2,1)S(1)}, bf16[1,768,768]{2,1,0:T(8,128)(2,1)}, u32[]{:S(2)}) copy-start(bf16[1,768,768]{2,1,0:T(8,128)(2,1)} %param.29) | copy-start | bytes 3538948
  7.2 57.3 %all-reduce.16.cloned.1.call-start = ((), (), s32[]{:S(2)}) async-start(), calls=%async_computation.10 | async-start | bytes 2359296 | tf_op jit(solution)/shard_map/psum | solution.py:144
  24.1 91.3 %all-reduce.18.cloned.1.call-start = ((), (), s32[]{:S(2)}) async-start(), calls=%async_computation.11 | async-start | bytes 2359296 | tf_op jit(solution)/shard_map/psum | solution.py:144
  25.7 97.4 %copy-start.96 = (s32[768,2]{0,1:T(2,128)}, s32[768,2]{0,1:T(2,128)S(1)}, u32[]{:S(2)}) copy-start(s32[768,2]{0,1:T(2,128)S(1)} %get-tuple-element.123) | copy-start | bytes 18436
  42.2 25.1 %copy-start.82 = (f32[768]{0:T(1024)}, f32[768]{0:T(1024)S(1)}, u32[]{:S(2)}) copy-start(f32[768]{0:T(1024)S(1)} %broadcast_multiply_fusion.3) | copy-start | bytes 9220
  88.0 17.5 copy-start.133
  105.5 13.8 copy-start.92
  142.6 9.1 copy-start.129
  142.7 110.0 %all-to-all-start.4 = ((bf16[8,384,768]{2,1,0:T(8,128)(2,1)}), bf16[8,384,768]{2,1,0:T(8,128)(2,1)}, u32[]{:S(2)}, u32[]{:S(2)}) async-start(bf16[8,384,768]{2,1,0:T(8,128)(2,1)} %bitcast.365), calls=%async_computation.4 | async-start | bytes 9437184 | tf_op jit(solution)/shard_map/all_to_all | solution.py:186
  148.3 11.4 copy-start.19
  252.6 108.5 %all-to-all-start.2 = ((bf16[8,384,768]{2,1,0:T(8,128)(2,1)}), bf16[8,384,768]{2,1,0:T(8,128)(2,1)}, u32[]{:S(2)}, u32[]{:S(2)}) async-start(bf16[8,384,768]{2,1,0:T(8,128)(2,1)} %bitcast.368), calls=%async_computation.2 | async-start | bytes 9437184 | tf_op jit(solution)/shard_map/all_to_all | solution.py:158
  361.1 108.5 %all-to-all-start = ((bf16[8,384,768]{2,1,0:T(8,128)(2,1)}), bf16[8,384,768]{2,1,0:T(8,128)(2,1)}, u32[]{:S(2)}, u32[]{:S(2)}) async-start(bf16[8,384,768]{2,1,0:T(8,128)(2,1)} %bitcast.366), calls=%async_computation | async-start | bytes 9437184 | tf_op jit(solution)/shard_map/all_to_all | solution.py:158
  369.7 7.0 copy-start.20
  369.7 7.0 copy-start.74
  369.7 7.4 copy-start.98
  469.6 108.3 %all-to-all-start.6 = ((bf16[8,384,768]{2,1,0:T(8,128)(2,1)}), bf16[8,384,768]{2,1,0:T(8,128)(2,1)}, u32[]{:S(2)}, u32[]{:S(2)}) async-start(bf16[8,384,768]{2,1,0:T(8,128)(2,1)} %bitcast.367), calls=%async_computation.6 | async-start | bytes 9437184 | tf_op jit(solution)/shard_map/all_to_all | solution.py:186
  474.2 447.4 %all-reduce.22.cloned.1.call-start = ((), (), s32[]{:S(2)}) async-start(), calls=%async_computation.15 | async-start | bytes 37748736 | tf_op jit(solution)/shard_map/psum | solution.py:166
  474.2 7.6 copy-start.139
  481.8 17.6 %copy-start.148 = (bf16[3072,768]{1,0:T(8,128)(2,1)}, bf16[3072,768]{1,0:T(8,128)(2,1)S(1)}, u32[]{:S(2)}) copy-start(bf16[3072,768]{1,0:T(8,128)(2,1)S(1)} %get-tuple-element.137) | copy-start | bytes 14155780
  921.6 110.1 %copy-start.33 = (bf16[8,384,768]{2,1,0:T(8,128)(2,1)S(1)}, bf16[8,384,768]{2,1,0:T(8,128)(2,1)}, u32[]{:S(2)}) copy-start(bf16[8,384,768]{2,1,0:T(8,128)(2,1)} %get-tuple-element.98) | copy-start | bytes 14155780
  921.6 217.8 %slice-start.8 = ((s8[4718592]{0:T(1024)(128)(4,1)}), s8[4194304]{0:T(1024)(128)(4,1)S(1)}, s32[]{:S(2)}) async-start(s8[4718592]{0:T(1024)(128)(4,1)} %bitcast.382), calls=%async_computation.24 | async-start | bytes 8388608
  1031.7 107.6 %slice-start.9 = ((s8[4718592]{0:T(1024)(128)(4,1)}), s8[524288]{0:T(1024)(128)(4,1)S(1)}, s32[]{:S(2)}) async-start(s8[4718592]{0:T(1024)(128)(4,1)} %bitcast.382), calls=%async_computation.25 | async-start | bytes 1048576
  1246.8 10.7 slice-start.6
  1246.8 108.3 %all-to-all-start.3 = ((bf16[8,384,768]{2,1,0:T(8,128)(2,1)}), bf16[8,384,768]{2,1,0:T(8,128)(2,1)}, u32[]{:S(2)}, u32[]{:S(2)}) async-start(bf16[8,384,768]{2,1,0:T(8,128)(2,1)} %get-tuple-element.96), calls=%async_computation.3 | async-start | bytes 9437184 | tf_op jit(solution)/shard_map/all_to_all | solution.py:167
  1251.6 398.7 %all-reduce.20.cloned.1.call-start = ((), (), s32[]{:S(2)}) async-start(), calls=%async_computation.14 | async-start | bytes 2359296 | tf_op jit(solution)/shard_map/psum | solution.py:264
  1252.3 7.7 slice-start.4
  1379.3 6.4 copy-start.13
  1379.3 6.4 copy-start.37
  1385.6 13.6 copy-start.67
  1385.7 13.6 copy-start.79
  1385.7 13.6 copy-start.91
  1385.7 13.7 copy-start.99
  1400.0 6.4 copy-start.11
  1400.0 6.4 copy-start.35
  1406.3 13.5 copy-start.65
  1406.3 13.5 copy-start.77
  1406.3 13.5 copy-start.89
  1406.4 13.6 copy-start.97
  1420.6 6.3 copy-start.26
  1440.5 12.6 copy-start.87
  1453.3 12.2 slice-start
  1471.7 6.3 copy-start.39
  1479.4 15.1 copy-start.94
  1501.4 153.2 %all-gather.5.cloned.1.call-start = ((), (), s32[]{:S(2)}) async-start(), calls=%async_computation.12 | async-start | bytes 5898240 | tf_op jit(solution)/shard_map/all_gather | solution.py:10
  1505.0 170.5 %all-gather.7.cloned.1.call-start = ((), (), s32[]{:S(2)}) async-start(), calls=%async_computation.13 | async-start | bytes 5898240 | tf_op jit(solution)/shard_map/all_gather | solution.py:10
  1527.4 77.3 %all-to-all-start.8 = ((bf16[8,2,36864]{2,1,0:T(2,128)(2,1)}), bf16[8,2,36864]{2,1,0:T(2,128)(2,1)}, u32[]{:S(2)}, u32[]{:S(2)}) async-start(bf16[8,2,36864]{2,1,0:T(2,128)(2,1)} %reshape.918), calls=%async_computation.8 | async-start | bytes 2359296 | tf_op jit(solution)/shard_map/all_to_all | solution.py:271
  1604.8 32.7 %all-to-all-start.9 = ((bf16[8,2,36864]{2,1,0:T(2,128)(2,1)}), bf16[8,2,36864]{2,1,0:T(2,128)(2,1)S(1)}, u32[]{:S(2)}, u32[]{:S(2)}) async-start(bf16[8,2,36864]{2,1,0:T(2,128)(2,1)} %reshape.920), calls=%async_computation.9 | async-start | bytes 2359296 | tf_op jit(solution)/shard_map/all_to_all | solution.py:278
  1683.3 50.1 %copy-start.95 = (f32[768]{0:T(1024)S(1)}, f32[768]{0:T(1024)}, u32[]{:S(2)}) copy-start(f32[768]{0:T(1024)} %copy-done.94) | copy-start | bytes 9220
  (124 other events, 389.6 us)
Sparse Core Ops, SparseCore 0:
  24.2 40.3 all-reduce.15
  77.6 37.7 all-reduce.17
  601.5 320.0 all-reduce.21
  1501.5 98.4 all-reduce.19
  1601.3 35.1 all-gather.4
  1638.0 37.4 all-gather.6
